TPU v7x, 32 devices: a whole 2x2x4 slice. The times are simulated.
32 devices in a mesh: groups: 2 (over y), sec: 2 (over x), row: 4 (over z), col: 2 (over core).
Axes of the slice: x: 2, y: 2, z: 4, core: 2. Of those that a mesh axis runs over, the one named last changes fastest.
Arguments:
- factors: bfloat16 [4, 2048, 2048], P(('groups', 'sec'), 'row', 'col'), parts along dimension 0, may hold values from -0.125 to 0.125
- inverses: bfloat16 [4, 2048, 2048], P(('groups', 'sec'), 'row', 'col'), parts along dimension 0, may hold values from -1.4 to 1.4, as said below
- sigma_end: float32 [4096, 2048], P(('groups', 'row'), 'col'), parts along dimension 0, may hold values from -1 to 6, as said below
Outputs:
- variance: float32 [4, 2048, 2048], P(('groups', 'sec'), 'row', 'col'), parts along dimension 0
There are 2 independent parts, one for each index of `groups`. A program takes and returns all parts, laid end to end along the dimension named above; each array names one. Nothing has to cross between parts.
Inputs may be any that keep to these rules, and one draw needn't show every extreme that they name: inverses[t] is lower triangular; its diagonal entries lie in 0.6 to 1.4. sigma_end is symmetric with diagonal entries in 2.5 to 6.
All inputs are finite; a program needn't handle non-finite values.
Results may differ from a plain program's by a relative error of at most 0.011.
Values may be sent and summed in bfloat16 or wider, within the bound.
A program may use at most 64 MiB of HBM per device.

v0:
```python
import jax
import jax.numpy as jnp
from jax import lax
from jax.sharding import PartitionSpec as P


def partner(shard, axis, stride):
    return lax.ppermute(shard, axis, [(i, i ^ 1 << stride) for i in range(lax.axis_size(axis))])


def passed_along(value, axis, steps):
    count = lax.axis_size(axis)
    first, last = (max(0, -steps), min(count, count - steps))
    return lax.ppermute(value, axis, [(source, source + steps) for source in range(first, last)])


def local(factors, inverses, sigma_end):
    row_size = lax.axis_size("row")
    col_size = lax.axis_size("col")
    sec_size = lax.axis_size("sec")
    row_index = lax.axis_index("row")
    col_index = lax.axis_index("col")
    sec_index = lax.axis_index("sec")
    _, tile_rows, _ = factors.shape
    per_column = row_size // col_size
    offset = row_index % per_column * tile_rows
    owns_panel = col_index == row_index // per_column

    def gather(tile):
        return lax.all_gather(tile, "row", axis=0, tiled=True)

    def left_of(full):
        mine = lax.dynamic_slice_in_dim(full, offset, tile_rows, 1)
        return jnp.where(owns_panel, mine, partner(mine, "col", 0))

    def cross(left, full):
        return lax.dot_general(
            left, full, (((0,), (0,)), ((), ())), preferred_element_type=jnp.float32
        )

    current = sigma_end.astype(jnp.bfloat16)
    factor = gather(factors[0])
    state = gather(current)
    inverse = gather(inverses[0])
    factor_left = left_of(factor)
    diagonal = cross(left_of(inverse), inverse)
    result = None
    for segment in range(sec_size):
        half = cross(factor_left, state).astype(jnp.bfloat16)
        whole = lax.all_gather(half, "col", axis=1, tiled=True)
        block = diagonal + jnp.dot(whole, factor, preferred_element_type=jnp.float32)
        active = sec_index == sec_size - 1 - segment
        result = block if result is None else jnp.where(active, block, result)
        if segment < sec_size - 1:
            state = gather(passed_along(block.astype(jnp.bfloat16), "sec", -1))
    return result[None]


def solution(mesh):
    in_specs = (
        P(("groups", "sec"), "row", "col"),
        P(("groups", "sec"), "row", "col"),
        P(("groups", "row"), "col"),
    )
    out_specs = P(("groups", "sec"), "row", "col")
    return jax.shard_map(local, mesh=mesh, in_specs=in_specs, out_specs=out_specs, check_vma=False)
```

profile of v0, /device:TPU:0, one launch (start us, length us, event | category | flops | bytes accessed | tf_op | source)
XLA Modules:
  0.0 415.6 jit_solution(8728628893357089546)
XLA Ops:
  6.5 0.7 all-gather.19.cloned.1.call-update
  7.3 0.7 all-gather.17.cloned.1.call-update
  8.0 0.0 all-gather.9.cloned.1.call-start
  8.1 2.8 convert_element_type.12
  10.8 0.0 all-gather.11.cloned.1.call-start
  10.9 81.5 %all-gather.19.cloned.1.call-done = bf16[1,2048,1024]{2,1,0:T(8,128)(2,1)} async-done(((bf16[1,512,1024]{2,1,0:T(8,128)(2,1)}), bf16[1,2048,1024]{2,1,0:T(8,128)(2,1)}) %all-gather.19.cloned.1.call-update) | async-done | bytes 4194320 | tf_op jit(solution)/shard_map/all_gather | solution.py:30
  92.4 1.7 dynamic-slice_bitcast_fusion
  94.2 0.1 collective-permute-start.1
  94.3 79.1 %all-gather.17.cloned.1.call-done = bf16[1,2048,1024]{2,1,0:T(8,128)(2,1)} async-done(((bf16[1,512,1024]{2,1,0:T(8,128)(2,1)}), bf16[1,2048,1024]{2,1,0:T(8,128)(2,1)}) %all-gather.17.cloned.1.call-update) | async-done | bytes 4194320 | tf_op jit(solution)/shard_map/all_gather | solution.py:30
  173.3 3.0 dynamic-slice_bitcast_fusion.1
  176.4 77.9 %all-gather.9.cloned.1.call-done = bf16[2048,1024]{1,0:T(8,128)(2,1)} async-done(((bf16[512,1024]{1,0:T(8,128)(2,1)}), bf16[2048,1024]{1,0:T(8,128)(2,1)}) %all-gather.9.cloned.1.call-update) | async-done | bytes 4194320 | tf_op jit(solution)/shard_map/all_gather | solution.py:30
  254.2 5.6 %convolution_convert_fusion.1 = bf16[512,1024]{1,0:T(8,128)(2,1)} fusion(bf16[2048,1024]{1,0:T(8,128)(2,1)} %all-gather.9.cloned.1.call-done, bf16[2048,512]{1,0:T(8,128)(2,1)S(1)} %dynamic-slice_bitcast_fusion, bf16[2048,512]{1,0:T(8,128)(2,1)} %collective-permute-done.1, pred[]{:T(512)S(6)} %eq.9), kind=kOutput, calls=%fused_computation.14 | convolution fusion | flops 2149056512 | bytes 9437185 | tf_op jit(solution)/shard_map/dot_general | solution.py:37
  259.8 0.0 all-gather.13.cloned.1.call-start
  259.9 6.6 %fusion.4 = f32[512,1024]{1,0:T(8,128)} fusion(bf16[1,2048,1024]{2,1,0:T(8,128)(2,1)} %all-gather.17.cloned.1.call-done, bf16[2048,512]{1,0:T(8,128)(2,1)} %dynamic-slice_bitcast_fusion.1, bf16[2048,512]{1,0:T(8,128)(2,1)} %collective-permute-done, pred[]{:T(512)S(6)} %eq.9), kind=kOutput, calls=%fused_computation.4 | convolution fusion | flops 2148532224 | bytes 10485761 | tf_op jit(solution)/shard_map/dot_general | solution.py:37
  266.4 3.2 all-gather.11.cloned.1.call-done
  269.7 7.1 %fusion.13 = (bf16[512,1024]{1,0:T(8,128)(2,1)S(1)}, f32[512,1024]{1,0:T(8,128)}) fusion(f32[512,1024]{1,0:T(8,128)} %fusion.4, bf16[512,2048]{1,0:T(8,128)(2,1)} %all-gather.11.cloned.1.call-done, bf16[1,2048,1024]{2,1,0:T(8,128)(2,1)} %all-gather.19.cloned.1.call-done), kind=kOutput, calls=%fused_computation.15 | convolution fusion | flops 2148532224 | bytes 11534336 | tf_op jit(solution)/shard_map/dot_general | solution.py:51
  276.8 1.3 collective-permute-start.2
  278.1 25.9 %collective-permute-done.2 = bf16[512,1024]{1,0:T(8,128)(2,1)S(1)} collective-permute-done((bf16[512,1024]{1,0:T(8,128)(2,1)S(1)}, bf16[512,1024]{1,0:T(8,128)(2,1)S(1)}, u32[]{:S(2)}, u32[]{:S(2)}) %collective-permute-start.2) | collective-permute-done | bytes 1048608 | tf_op jit(solution)/shard_map/ppermute | solution.py:14
  304.0 1.0 copy-done
  305.0 0.0 all-gather.15.cloned.1.call-start
  305.0 81.2 %all-gather.13.cloned.1.call-done = bf16[2048,1024]{1,0:T(8,128)(2,1)} async-done(((bf16[512,1024]{1,0:T(8,128)(2,1)}), bf16[2048,1024]{1,0:T(8,128)(2,1)}) %all-gather.13.cloned.1.call-update) | async-done | bytes 4194320 | tf_op jit(solution)/shard_map/all_gather | solution.py:30
  386.3 5.5 %convolution_convert_fusion = bf16[512,1024]{1,0:T(8,128)(2,1)} fusion(bf16[2048,1024]{1,0:T(8,128)(2,1)} %all-gather.13.cloned.1.call-done, bf16[2048,512]{1,0:T(8,128)(2,1)S(1)} %dynamic-slice_bitcast_fusion, bf16[2048,512]{1,0:T(8,128)(2,1)} %collective-permute-done.1, pred[]{:T(512)S(6)} %eq.9), kind=kOutput, calls=%fused_computation.13 | convolution fusion | flops 2149056512 | bytes 9437185 | tf_op jit(solution)/shard_map/dot_general | solution.py:37
  391.8 9.9 %all-gather.15.cloned.1.call-done = bf16[512,2048]{1,0:T(8,128)(2,1)} async-done(((bf16[512,1024]{1,0:T(8,128)(2,1)}), bf16[512,2048]{1,0:T(8,128)(2,1)}) %all-gather.15.cloned.1.call-update) | async-done | bytes 2097168 | tf_op jit(solution)/shard_map/all_gather | solution.py:50
  401.7 7.1 %select_bitcast_fusion = f32[1,512,1024]{2,1,0:T(8,128)} fusion(f32[512,1024]{1,0:T(8,128)} %get-tuple-element.6, f32[512,1024]{1,0:T(8,128)} %fusion.4, bf16[512,2048]{1,0:T(8,128)(2,1)} %all-gather.15.cloned.1.call-done, bf16[1,2048,1024]{2,1,0:T(8,128)(2,1)} %all-gather.19.cloned.1.call-done, pred[]{:T(512)S(6)} %eq.8), kind=kOutput, calls=%fused_computation.8 | convolution fusion | flops 2148532224 | bytes 12582913 | tf_op jit(solution)/shard_map/dot_general | solution.py:51
  (10 shorter events, 0.1 us)
Async XLA Ops:
  6.5 85.9 %all-gather.19.cloned.1.call-start = ((), (), s32[]{:S(2)}) async-start(), calls=%async_computation.5 | async-start | bytes 5242880 | tf_op jit(solution)/shard_map/all_gather | solution.py:30
  7.3 166.1 %all-gather.17.cloned.1.call-start = ((), (), s32[]{:S(2)}) async-start(), calls=%async_computation.4 | async-start | bytes 5242880 | tf_op jit(solution)/shard_map/all_gather | solution.py:30
  8.0 246.2 %all-gather.9.cloned.1.call-start = ((), (), s32[]{:S(2)}) async-start(), calls=%async_computation | async-start | bytes 5242880 | tf_op jit(solution)/shard_map/all_gather | solution.py:30
  10.8 258.9 %all-gather.11.cloned.1.call-start = ((), (), s32[]{:S(2)}) async-start(), calls=%async_computation.1 | async-start | bytes 3145728 | tf_op jit(solution)/shard_map/all_gather | solution.py:50
  94.2 160.1 %collective-permute-start.1 = (bf16[2048,512]{1,0:T(8,128)(2,1)S(1)}, bf16[2048,512]{1,0:T(8,128)(2,1)}, u32[]{:S(2)}, u32[]{:S(2)}) collective-permute-start(bf16[2048,512]{1,0:T(8,128)(2,1)S(1)} %dynamic-slice_bitcast_fusion), channel_id=1, source_target_pairs={{0,1},{1,0},{2,3},{3,2},{4,5},{5,4},{6,7},{7,6},{8,9},{9,8},{10,11... | collective-permute-start | bytes 6291464 | tf_op jit(solution)/shard_map/ppermute | solution.py:8
  176.4 83.5 %collective-permute-start = (bf16[2048,512]{1,0:T(8,128)(2,1)}, bf16[2048,512]{1,0:T(8,128)(2,1)}, u32[]{:S(2)}, u32[]{:S(2)}) collective-permute-start(bf16[2048,512]{1,0:T(8,128)(2,1)} %dynamic-slice_bitcast_fusion.1), channel_id=1, source_target_pairs={{0,1},{1,0},{2,3},{3,2},{4,5},{5,4},{6,7},{7,6},{8,9},{9,8},{10,11... | collective-permute-start | bytes 6291464 | tf_op jit(solution)/shard_map/ppermute | solution.py:8
  259.8 126.5 %all-gather.13.cloned.1.call-start = ((), (), s32[]{:S(2)}) async-start(), calls=%async_computation.2 | async-start | bytes 5242880 | tf_op jit(solution)/shard_map/all_gather | solution.py:30
  276.8 27.2 %collective-permute-start.2 = (bf16[512,1024]{1,0:T(8,128)(2,1)S(1)}, bf16[512,1024]{1,0:T(8,128)(2,1)S(1)}, u32[]{:S(2)}, u32[]{:S(2)}) collective-permute-start(bf16[512,1024]{1,0:T(8,128)(2,1)S(1)} %get-tuple-element.5), channel_id=1, source_target_pairs={{8,0},{9,1},{10,2},{11,3},{12,4},{13,5},{14,6},{15,7},{24,16},{25,... | collective-permute-start | bytes 3145736 | tf_op jit(solution)/shard_map/ppermute | solution.py:14
  304.0 1.0 copy-start
  305.0 96.7 %all-gather.15.cloned.1.call-start = ((), (), s32[]{:S(2)}) async-start(), calls=%async_computation.3 | async-start | bytes 3145728 | tf_op jit(solution)/shard_map/all_gather | solution.py:50
Sparse Core Ops, SparseCore 0:
  8.9 83.4 all-gather.18
  94.0 79.2 all-gather.16
  174.9 79.2 all-gather.8
  259.9 9.7 all-gather.10
  305.1 81.1 all-gather.12
  391.9 9.7 all-gather.14
where the time goes:
time: 416 us
  waiting for transfers between devices  360 us (87%)
  matrix products  31.9 us (8%)
  between operations  13.5 us (3%)
  local copies, waits for them, and re-layouts  5.75 us (1%)
    all_gather x4, waiting for transfers between devices, gather(): return lax.all_gather(tile, 'row', axis=0, tiled=True)  320 us
    ppermute x1, waiting for transfers between devices, passed_along(): lax.ppermute(value, axis, [(source, source + steps) for source in range(f...  25.9 us
    dot_general x3, matrix products, cross(): lax.dot_general(left, full, (((0,), (0,)), ((), ())), preferred_element_t...  17.7 us
    dot_general x2, matrix products, local(): jnp.dot(whole, factor, preferred_element_type=jnp.float32)  14.2 us
    all_gather x2, waiting for transfers between devices, local(): whole = lax.all_gather(half, 'col', axis=1, tiled=True)  13.1 us
  transfers between devices with their start and end apart: 9, of which 7 were waited for; matrix products, arithmetic and copies ran while one was open for 5% of the time, Pallas kernels for 0%

commit v1 on v0

--- a/solution.py
+++ b/solution.py
@@ -2,6 +2,18 @@
 import jax.numpy as jnp
 from jax import lax
 from jax.sharding import PartitionSpec as P
+
+
+def collect(x, axis, dim):
+    ways, here = (lax.axis_size(axis), lax.axis_index(axis))
+    grown, reach = (x, 1)
+    while reach < ways:
+        theirs = lax.ppermute(grown, axis, [(d, d ^ reach) for d in range(ways)])
+        mine_first = jnp.concatenate([grown, theirs], axis=dim)
+        theirs_first = jnp.concatenate([theirs, grown], axis=dim)
+        grown = jnp.where(here & reach == 0, mine_first, theirs_first)
+        reach = 2 * reach
+    return grown
 
 
 def partner(shard, axis, stride):
@@ -27,7 +39,7 @@
     owns_panel = col_index == row_index // per_column
 
     def gather(tile):
-        return lax.all_gather(tile, "row", axis=0, tiled=True)
+        return collect(tile, "row", 0)
 
     def left_of(full):
         mine = lax.dynamic_slice_in_dim(full, offset, tile_rows, 1)

time: 416 us -> 510 us (1.23)
  waiting for transfers between devices: 360 us -> 421 us
  other arithmetic: 2.75 us -> 20.1 us
  starting transfers between devices: 1.56 us -> 18.8 us
    ppermute x0 -> x8, waiting for transfers between devices: none -> 377 us  [collect(): theirs = lax.ppermute(grown, axis, [(d, d ^ reach) for d in range(ways)])]
    all_gather x4 -> x0, waiting for transfers between devices: 320 us -> none  [gather(): return lax.all_gather(tile, 'row', axis=0, tiled=True)]
    select_n x0 -> x6, other arithmetic: none -> 19.9 us  [collect(): grown = jnp.where(here & reach == 0, mine_first, theirs_first)]
    ppermute x0 -> x8, starting transfers between devices: none -> 17.3 us  [collect(): theirs = lax.ppermute(grown, axis, [(d, d ^ reach) for d in range(ways)])]
  transfers between devices with their start and end apart: 9 -> 13, of which waited for: 7 -> 11; matrix products, arithmetic and copies ran while one was open for 5% -> 6% of each run, Pallas kernels for 0% -> 0%
where the time goes in v1:
time: 510 us; the launch traced here: 509 us
  waiting for transfers between devices  421 us (83%)
  matrix products  31.3 us (6%)
  other arithmetic  20.1 us (4%)
  starting transfers between devices  18.8 us (4%)
  between operations  13.5 us (3%)
    ppermute x8, waiting for transfers between devices, collect(): theirs = lax.ppermute(grown, axis, [(d, d ^ reach) for d in range(ways)])  377 us
    ppermute x1, waiting for transfers between devices, passed_along(): lax.ppermute(value, axis, [(source, source + steps) for source in range(f...  25.9 us
    select_n x6, other arithmetic, collect(): grown = jnp.where(here & reach == 0, mine_first, theirs_first)  19.9 us
    all_gather x2, waiting for transfers between devices, local(): whole = lax.all_gather(half, 'col', axis=1, tiled=True)  17.8 us
    ppermute x8, starting transfers between devices, collect(): theirs = lax.ppermute(grown, axis, [(d, d ^ reach) for d in range(ways)])  17.3 us
    dot_general x3, matrix products, cross(): lax.dot_general(left, full, (((0,), (0,)), ((), ())), preferred_element_t...  17.1 us
    dot_general x2, matrix products, local(): jnp.dot(whole, factor, preferred_element_type=jnp.float32)  14.2 us
  transfers between devices with their start and end apart: 13, of which 11 were waited for; matrix products, arithmetic and copies ran while one was open for 6% of the time, Pallas kernels for 0%

profile of v1, /device:TPU:0, one launch (start us, length us, event | category | flops | bytes accessed | tf_op | source)
XLA Modules:
  0.0 509.4 jit_solution(18293130368099282647)
XLA Ops:
  6.5 3.0 collective-permute-start.3
  9.6 23.4 %collective-permute-done.3 = bf16[512,1024]{1,0:T(8,128)(2,1)S(1)} collective-permute-done((bf16[512,1024]{1,0:T(8,128)(2,1)}, bf16[512,1024]{1,0:T(8,128)(2,1)S(1)}, u32[]{:S(2)}, u32[]{:S(2)}) %collective-permute-start.3) | collective-permute-done | bytes 1048608 | tf_op jit(solution)/shard_map/ppermute | solution.py:11
  32.9 2.7 maximum_select_fusion.7
  35.6 2.8 collective-permute-start.4
  40.7 66.4 %collective-permute-done = bf16[512,1024]{1,0:T(8,128)(2,1)} collective-permute-done((bf16[512,1024]{1,0:T(8,128)(2,1)}, bf16[512,1024]{1,0:T(8,128)(2,1)}, u32[]{:S(2)}, u32[]{:S(2)}) %collective-permute-start) | collective-permute-done | bytes 1048608 | tf_op jit(solution)/shard_map/ppermute | solution.py:11
  107.1 4.7 maximum_select_fusion.6
  114.1 15.3 %collective-permute-done.6 = bf16[512,1024]{1,0:T(8,128)(2,1)} collective-permute-done((bf16[512,1024]{1,0:T(8,128)(2,1)S(1)}, bf16[512,1024]{1,0:T(8,128)(2,1)}, u32[]{:S(2)}, u32[]{:S(2)}) %collective-permute-start.6) | collective-permute-done | bytes 1048608 | tf_op jit(solution)/shard_map/ppermute | solution.py:11
  129.5 3.9 maximum_select_fusion.8
  135.8 83.6 %collective-permute-done.4 = bf16[1024,1024]{1,0:T(8,128)(2,1)} collective-permute-done((bf16[1024,1024]{1,0:T(8,128)(2,1)S(1)}, bf16[1024,1024]{1,0:T(8,128)(2,1)}, u32[]{:S(2)}, u32[]{:S(2)}) %collective-permute-start.4) | collective-permute-done | bytes 2097184 | tf_op jit(solution)/shard_map/ppermute | solution.py:11
  219.4 3.5 maximum_select_fusion.1
  224.9 39.5 %collective-permute-done.1 = bf16[1024,1024]{1,0:T(8,128)(2,1)} collective-permute-done((bf16[1024,1024]{1,0:T(8,128)(2,1)}, bf16[1024,1024]{1,0:T(8,128)(2,1)}, u32[]{:S(2)}, u32[]{:S(2)}) %collective-permute-start.1) | collective-permute-done | bytes 2097184 | tf_op jit(solution)/shard_map/ppermute | solution.py:11
  264.4 4.2 maximum_select_fusion
  271.2 37.1 %collective-permute-done.7 = bf16[1024,1024]{1,0:T(8,128)(2,1)} collective-permute-done((bf16[1024,1024]{1,0:T(8,128)(2,1)}, bf16[1024,1024]{1,0:T(8,128)(2,1)}, u32[]{:S(2)}, u32[]{:S(2)}) %collective-permute-start.7) | collective-permute-done | bytes 2097184 | tf_op jit(solution)/shard_map/ppermute | solution.py:11
  308.3 7.0 %fusion.18 = bf16[512,1024]{1,0:T(8,128)(2,1)} fusion(bf16[1024,1024]{1,0:T(8,128)(2,1)} %collective-permute-done.7, bf16[1024,1024]{1,0:T(8,128)(2,1)} %maximum_select_fusion.8, pred[]{:T(512)S(6)} %eq.22, bf16[2048,512]{1,0:T(8,128)(2,1)S(1)} %constant_dynamic-slice_fusion, bf16[2048,512]{1,0:T(8,128)(2,1)} %collective-permute-done.5, pred[]{:T(512)S(6)} %eq.11), kind=kOutput, calls=%fused_computation.29 | convolution fusion | flops 2167930880 | bytes 9437186 | tf_op jit(solution)/shard_map/dot_general | solution.py:49
  315.6 6.5 %fusion.14 = f32[512,1024]{1,0:T(8,128)} fusion(bf16[2048,1024]{1,0:T(8,128)(2,1)} %copy-done.1, bf16[2048,512]{1,0:T(8,128)(2,1)} %constant_dynamic-slice_fusion.1, bf16[2048,512]{1,0:T(8,128)(2,1)} %collective-permute-done.2, pred[]{:T(512)S(6)} %eq.11), kind=kOutput, calls=%fused_computation.23 | convolution fusion | flops 2148532224 | bytes 10485761 | tf_op jit(solution)/shard_map/dot_general | solution.py:49
  322.1 5.3 %all-gather.3.cloned.1.call-done = bf16[512,2048]{1,0:T(8,128)(2,1)} async-done(((bf16[512,1024]{1,0:T(8,128)(2,1)}), bf16[512,2048]{1,0:T(8,128)(2,1)}) %all-gather.3.cloned.1.call-update) | async-done | bytes 2097168 | tf_op jit(solution)/shard_map/all_gather | solution.py:62
  327.4 7.1 %fusion.21 = (bf16[512,1024]{1,0:T(8,128)(2,1)S(1)}, f32[512,1024]{1,0:T(8,128)}) fusion(f32[512,1024]{1,0:T(8,128)} %fusion.14, bf16[512,2048]{1,0:T(8,128)(2,1)} %all-gather.3.cloned.1.call-done, bf16[2048,1024]{1,0:T(8,128)(2,1)} %copy-done), kind=kOutput, calls=%fused_computation.34 | convolution fusion | flops 2148532224 | bytes 11534336 | tf_op jit(solution)/shard_map/dot_general | solution.py:63
  335.8 25.9 %collective-permute-done.8 = bf16[512,1024]{1,0:T(8,128)(2,1)S(1)} collective-permute-done((bf16[512,1024]{1,0:T(8,128)(2,1)S(1)}, bf16[512,1024]{1,0:T(8,128)(2,1)S(1)}, u32[]{:S(2)}, u32[]{:S(2)}) %collective-permute-start.8) | collective-permute-done | bytes 1048608 | tf_op jit(solution)/shard_map/ppermute | solution.py:26
  363.5 22.8 %collective-permute-done.9 = bf16[512,1024]{1,0:T(8,128)(2,1)S(1)} collective-permute-done((bf16[512,1024]{1,0:T(8,128)(2,1)S(1)}, bf16[512,1024]{1,0:T(8,128)(2,1)S(1)}, u32[]{:S(2)}, u32[]{:S(2)}) %collective-permute-start.9) | collective-permute-done | bytes 1048608 | tf_op jit(solution)/shard_map/ppermute | solution.py:11
  387.4 2.7 collective-permute-start.10
  390.1 89.4 %collective-permute-done.10 = bf16[1024,1024]{1,0:T(8,128)(2,1)S(1)} collective-permute-done((bf16[1024,1024]{1,0:T(8,128)(2,1)S(1)}, bf16[1024,1024]{1,0:T(8,128)(2,1)S(1)}, u32[]{:S(2)}, u32[]{:S(2)}) %collective-permute-start.10) | collective-permute-done | bytes 2097184 | tf_op jit(solution)/shard_map/ppermute | solution.py:11
  479.5 3.5 fusion.17
  483.0 12.5 %all-gather.5.cloned.1.call-done = bf16[512,2048]{1,0:T(8,128)(2,1)} async-done(((bf16[512,1024]{1,0:T(8,128)(2,1)}), bf16[512,2048]{1,0:T(8,128)(2,1)}) %all-gather.5.cloned.1.call-update) | async-done | bytes 2097168 | tf_op jit(solution)/shard_map/all_gather | solution.py:62
  495.5 7.1 %select_bitcast_fusion = f32[1,512,1024]{2,1,0:T(8,128)} fusion(f32[512,1024]{1,0:T(8,128)} %get-tuple-element.6, f32[512,1024]{1,0:T(8,128)} %fusion.14, bf16[512,2048]{1,0:T(8,128)(2,1)} %all-gather.5.cloned.1.call-done, bf16[2048,1024]{1,0:T(8,128)(2,1)} %copy-done, pred[]{:T(512)S(6)} %eq.10), kind=kOutput, calls=%fused_computation.22 | convolution fusion | flops 2148532224 | bytes 12582913 | tf_op jit(solution)/shard_map/dot_general | solution.py:63
  (24 shorter events, 16.0 us)
Async XLA Ops:
  6.5 320.9 %all-gather.3.cloned.1.call-start = ((), (), s32[]{:S(2)}) async-start(), calls=%async_computation | async-start | bytes 3145728 | tf_op jit(solution)/shard_map/all_gather | solution.py:62
  6.5 26.4 %collective-permute-start.3 = (bf16[512,1024]{1,0:T(8,128)(2,1)}, bf16[512,1024]{1,0:T(8,128)(2,1)S(1)}, u32[]{:S(2)}, u32[]{:S(2)}) collective-permute-start(bf16[512,1024]{1,0:T(8,128)(2,1)} %bitcast.9), channel_id=1, source_target_pairs={{0,2},{2,0},{4,6},{6,4},{1,3},{3,1},{5,7},{7,5},{8,10},{10,8},{12,... | collective-permute-start | bytes 3145736 | tf_op jit(solution)/shard_map/ppermute | solution.py:11
  9.6 30.5 %copy-start.2 = (f32[512,1024]{1,0:T(8,128)S(1)}, f32[512,1024]{1,0:T(8,128)}, u32[]{:S(2)}) copy-start(f32[512,1024]{1,0:T(8,128)} %param.5) | copy-start | bytes 6291460
  35.6 183.8 %collective-permute-start.4 = (bf16[1024,1024]{1,0:T(8,128)(2,1)S(1)}, bf16[1024,1024]{1,0:T(8,128)(2,1)}, u32[]{:S(2)}, u32[]{:S(2)}) collective-permute-start(bf16[1024,1024]{1,0:T(8,128)(2,1)S(1)} %maximum_select_fusion.7), channel_id=1, source_target_pairs={{0,4},{2,6},{4,0},{6,2},{1,5},{3,7},{5,1},{7,3},{8,12},{10,14},{12... | collective-permute-start | bytes 6291464 | tf_op jit(solution)/shard_map/ppermute | solution.py:11
  38.5 68.7 %collective-permute-start = (bf16[512,1024]{1,0:T(8,128)(2,1)}, bf16[512,1024]{1,0:T(8,128)(2,1)}, u32[]{:S(2)}, u32[]{:S(2)}) collective-permute-start(bf16[512,1024]{1,0:T(8,128)(2,1)} %bitcast), channel_id=1, source_target_pairs={{0,2},{2,0},{4,6},{6,4},{1,3},{3,1},{5,7},{7,5},{8,10},{10,8},{12,... | collective-permute-start | bytes 3145736 | tf_op jit(solution)/shard_map/ppermute | solution.py:11
  40.2 89.3 %collective-permute-start.6 = (bf16[512,1024]{1,0:T(8,128)(2,1)S(1)}, bf16[512,1024]{1,0:T(8,128)(2,1)}, u32[]{:S(2)}, u32[]{:S(2)}) collective-permute-start(bf16[512,1024]{1,0:T(8,128)(2,1)S(1)} %convert_element_type.12), channel_id=1, source_target_pairs={{0,2},{2,0},{4,6},{6,4},{1,3},{3,1},{5,7},{7,5},{8,10},{10,8},{12,... | collective-permute-start | bytes 3145736 | tf_op jit(solution)/shard_map/ppermute | solution.py:11
  111.8 152.6 %collective-permute-start.1 = (bf16[1024,1024]{1,0:T(8,128)(2,1)}, bf16[1024,1024]{1,0:T(8,128)(2,1)}, u32[]{:S(2)}, u32[]{:S(2)}) collective-permute-start(bf16[1024,1024]{1,0:T(8,128)(2,1)} %maximum_select_fusion.6), channel_id=1, source_target_pairs={{0,4},{2,6},{4,0},{6,2},{1,5},{3,7},{5,1},{7,3},{8,12},{10,14},{12... | collective-permute-start | bytes 6291464 | tf_op jit(solution)/shard_map/ppermute | solution.py:11
  133.3 174.9 %collective-permute-start.7 = (bf16[1024,1024]{1,0:T(8,128)(2,1)}, bf16[1024,1024]{1,0:T(8,128)(2,1)}, u32[]{:S(2)}, u32[]{:S(2)}) collective-permute-start(bf16[1024,1024]{1,0:T(8,128)(2,1)} %maximum_select_fusion.8), channel_id=1, source_target_pairs={{0,4},{2,6},{4,0},{6,2},{1,5},{3,7},{5,1},{7,3},{8,12},{10,14},{12... | collective-permute-start | bytes 6291464 | tf_op jit(solution)/shard_map/ppermute | solution.py:11
  222.9 1.9 copy-start
  224.9 83.4 %collective-permute-start.5 = (bf16[2048,512]{1,0:T(8,128)(2,1)S(1)}, bf16[2048,512]{1,0:T(8,128)(2,1)}, u32[]{:S(2)}, u32[]{:S(2)}) collective-permute-start(bf16[2048,512]{1,0:T(8,128)(2,1)S(1)} %constant_dynamic-slice_fusion), channel_id=1, source_target_pairs={{0,1},{1,0},{2,3},{3,2},{4,5},{5,4},{6,7},{7,6},{8,9},{9,8},{10,11... | collective-permute-start | bytes 6291464 | tf_op jit(solution)/shard_map/ppermute | solution.py:20
  268.6 2.6 copy-start.1
  271.2 44.4 %collective-permute-start.2 = (bf16[2048,512]{1,0:T(8,128)(2,1)}, bf16[2048,512]{1,0:T(8,128)(2,1)}, u32[]{:S(2)}, u32[]{:S(2)}) collective-permute-start(bf16[2048,512]{1,0:T(8,128)(2,1)} %constant_dynamic-slice_fusion.1), channel_id=1, source_target_pairs={{0,1},{1,0},{2,3},{3,2},{4,5},{5,4},{6,7},{7,6},{8,9},{9,8},{10,11... | collective-permute-start | bytes 6291464 | tf_op jit(solution)/shard_map/ppermute | solution.py:20
  315.3 180.1 %all-gather.5.cloned.1.call-start = ((), (), s32[]{:S(2)}) async-start(), calls=%async_computation.1 | async-start | bytes 3145728 | tf_op jit(solution)/shard_map/all_gather | solution.py:62
  334.6 27.2 %collective-permute-start.8 = (bf16[512,1024]{1,0:T(8,128)(2,1)S(1)}, bf16[512,1024]{1,0:T(8,128)(2,1)S(1)}, u32[]{:S(2)}, u32[]{:S(2)}) collective-permute-start(bf16[512,1024]{1,0:T(8,128)(2,1)S(1)} %get-tuple-element.5), channel_id=1, source_target_pairs={{8,0},{9,1},{10,2},{11,3},{12,4},{13,5},{14,6},{15,7},{24,16},{25,... | collective-permute-start | bytes 3145736 | tf_op jit(solution)/shard_map/ppermute | solution.py:26
  361.7 24.6 %collective-permute-start.9 = (bf16[512,1024]{1,0:T(8,128)(2,1)S(1)}, bf16[512,1024]{1,0:T(8,128)(2,1)S(1)}, u32[]{:S(2)}, u32[]{:S(2)}) collective-permute-start(bf16[512,1024]{1,0:T(8,128)(2,1)S(1)} %collective-permute-done.8), channel_id=1, source_target_pairs={{0,2},{2,0},{4,6},{6,4},{1,3},{3,1},{5,7},{7,5},{8,10},{10,8},{12,... | collective-permute-start | bytes 3145736 | tf_op jit(solution)/shard_map/ppermute | solution.py:11
  387.4 92.1 %collective-permute-start.10 = (bf16[1024,1024]{1,0:T(8,128)(2,1)S(1)}, bf16[1024,1024]{1,0:T(8,128)(2,1)S(1)}, u32[]{:S(2)}, u32[]{:S(2)}) collective-permute-start(bf16[1024,1024]{1,0:T(8,128)(2,1)S(1)} %maximum_select_fusion.9), channel_id=1, source_target_pairs={{0,4},{2,6},{4,0},{6,2},{1,5},{3,7},{5,1},{7,3},{8,12},{10,14},{12... | collective-permute-start | bytes 6291464 | tf_op jit(solution)/shard_map/ppermute | solution.py:11
Sparse Core Ops, SparseCore 0:
  315.5 11.9 all-gather.2
  483.1 12.2 all-gather.4
